TPU v7x, 32 devices: a whole 2x2x4 slice. The times are simulated.
32 devices in a mesh: dp: 4 (over x, core), seq: 8 (over z, y).
Axes of the slice: x: 2, y: 2, z: 4, core: 2. Of those that a mesh axis runs over, the one named last changes fastest.
Arguments:
- spatial_input: bfloat16 [4, 8, 64, 256], P('dp', 'seq'), may hold values from -6 to 6
- temporal_input: bfloat16 [4, 64, 8, 256], P('dp', 'seq'), may hold values from -6 to 6
- out_cotangent: bfloat16 [4, 8, 64, 256], P('dp', 'seq'), may hold values from -6 to 6
- weights: bfloat16 [2, 256, 1024], replicated, may hold values from -3 to 3
- gains: float32 [2, 256], replicated, may hold values from 0.1 to 1.9
Outputs:
- input_grad: bfloat16 [4, 8, 64, 256], P('dp', 'seq')
- weight_grads: float32 [2, 262144], P(None, ('dp', 'seq'))
- gain_grads: float32 [2, 256], replicated
All inputs are finite; a program needn't handle non-finite values.
Results may differ from a plain program's by a relative error of at most 0.023.
Values may be sent and summed in bfloat16 or wider, within the bound.
A program may use at most 64 MiB of HBM per device.

v0:
```python
from functools import partial
import math
import jax
import jax.numpy as jnp
from jax import lax
from jax.sharding import PartitionSpec as P

HEADS = 4


def one_head(head_parts, score_scale):
    query_rows, key_rows, value_rows = head_parts
    scores = (
        jnp.einsum("gqe,gke->gqk", query_rows, key_rows, preferred_element_type=jnp.float32)
        * score_scale
    )
    probs = jax.nn.softmax(scores, axis=-1).astype(jnp.bfloat16)
    return jnp.einsum("gqk,gke->gqe", probs, value_rows, preferred_element_type=jnp.float32).astype(
        jnp.bfloat16
    )


def attend_block(block_input, gain_vector, weight, head_count):
    groups, length, model_width = block_input.shape
    head_size = model_width // head_count
    mean_sq = jnp.mean(block_input * block_input, axis=-1, keepdims=True)
    normed = (block_input * lax.rsqrt(mean_sq + 1e-06) * gain_vector).astype(jnp.bfloat16)
    w_cast = weight.astype(jnp.bfloat16)
    packed = jnp.dot(
        normed.reshape(groups * length, model_width),
        w_cast[:, : 3 * model_width],
        preferred_element_type=jnp.float32,
    ).astype(jnp.bfloat16)
    packed = jnp.transpose(
        packed.reshape(groups, length, 3, head_count, head_size), (2, 3, 0, 1, 4)
    )
    head_fn = jax.checkpoint(partial(one_head, score_scale=1.0 / math.sqrt(head_size)))
    mixed_heads = lax.map(head_fn, (packed[0], packed[1], packed[2]))
    mixed_heads = jnp.transpose(mixed_heads, (1, 2, 0, 3)).reshape(groups * length, model_width)
    result = jnp.dot(mixed_heads, w_cast[:, 3 * model_width :], preferred_element_type=jnp.float32)
    return result.reshape(groups, length, model_width)


def per_device(spatial_input, temporal_input, out_cotangent, weights, gains):
    w_float = weights.astype(jnp.float32)
    block_fn = partial(attend_block, head_count=HEADS)
    sample_count = spatial_input.shape[0] * lax.axis_size("dp")
    frame_count = spatial_input.shape[1] * lax.axis_size("seq")
    patch_count = spatial_input.shape[2]
    grad_factor = 1.0 / math.sqrt(sample_count * frame_count * patch_count)
    patch_major = jnp.swapaxes(out_cotangent[0], 0, 1)
    temporal_cot = lax.all_to_all(
        patch_major, "seq", split_axis=0, concat_axis=1, tiled=True
    ).astype(jnp.float32)
    unused_t, pullback_t = jax.vjp(
        block_fn, temporal_input[0].astype(jnp.float32), gains[1], w_float[1]
    )
    grad_ut, grad_gt, grad_wt = pullback_t(temporal_cot)
    temporal_term = (grad_wt * grad_factor).reshape(1, -1)
    mid_grad = (temporal_cot + grad_ut).astype(jnp.bfloat16)
    frame_back = lax.all_to_all(mid_grad, "seq", split_axis=1, concat_axis=0, tiled=True)
    spatial_cot = jnp.swapaxes(frame_back, 0, 1).astype(jnp.float32)
    unused_s, pullback_s = jax.vjp(
        block_fn, spatial_input[0].astype(jnp.float32), gains[0], w_float[0]
    )
    grad_us, grad_gs, grad_ws = pullback_s(spatial_cot)
    input_grad = (spatial_cot + grad_us).astype(jnp.bfloat16)[None]
    spatial_term = (grad_ws * grad_factor).reshape(1, -1)
    both_terms = jnp.concatenate([spatial_term, temporal_term], axis=0)
    grid_terms = both_terms.reshape(2, lax.axis_size("dp"), lax.axis_size("seq"), -1)
    over_frames = lax.psum_scatter(
        grid_terms.astype(jnp.bfloat16), "seq", scatter_dimension=2, tiled=True
    ).astype(jnp.float32)
    over_frames = over_frames.reshape(2, lax.axis_size("dp"), -1)
    weight_grads = (
        lax.psum_scatter(over_frames.astype(jnp.bfloat16), "dp", scatter_dimension=1, tiled=True)
        .astype(jnp.float32)
        .reshape(2, -1)
    )
    gain_grads = lax.psum(jnp.stack([grad_gs, grad_gt]) * grad_factor, ("dp", "seq"))
    return (input_grad, weight_grads, gain_grads)


def solution(mesh):
    return jax.shard_map(
        per_device,
        mesh=mesh,
        in_specs=(
            P("dp", "seq", None, None),
            P("dp", "seq", None, None),
            P("dp", "seq", None, None),
            P(),
            P(),
        ),
        out_specs=(P("dp", "seq", None, None), P(None, ("dp", "seq")), P()),
        check_vma=False,
    )
```

profile of v0, /device:TPU:0, one launch (start us, length us, event | category | flops | bytes accessed | tf_op | source)
XLA Modules:
  0.0 179.6 jit_solution(7019148246470243943)
XLA Ops:
  7.2 0.5 broadcast.288
  7.7 1.4 reduce.34
  9.1 0.6 reshape.395
  9.7 7.4 %all-to-all-start = ((bf16[8,2,1024]{2,1,0:T(2,128)(2,1)}), bf16[8,2,1024]{2,1,0:T(2,128)(2,1)S(1)}, u32[]{:S(2)}, u32[]{:S(2)}) async-start(bf16[8,2,1024]{2,1,0:T(2,128)(2,1)} %reshape.395), calls=%async_computation | async-start | bytes 65536 | tf_op jit(solution)/shard_map/all_to_all | solution.py:52
  17.3 0.7 copy-done.1
  18.1 0.6 copy-done.2
  18.9 1.3 slice_bitcast_fusion.1
  20.6 2.0 %while.59 = (s32[]{:T(128)}, bf16[4,8,8,64]{3,2,1,0:T(8,128)(2,1)S(1)}, bf16[4,8,8,64]{3,2,1,0:T(8,128)(2,1)S(1)}, bf16[4,8,8,64]{3,2,1,0:T(8,128)(2,1)S(1)}, bf16[4,8,8,64]{3,2,1,0:T(8,128)(2,1)S(1)}, /*index=5*/s32[]{:T(128)}) while((s32[]{:T(128)}, bf16[4,8,8,64]{3,2,1,0:T(8,128)(2,1)S(1)}, bf16[4,8,8,64]{3,2,1,0:T(8,128)(2,1)S(1)}, ...), condition=%wide.region_21.22_spmd, body=%wide.region_18.0_spmd.sunk | while | flops 204368 | bytes 105805 | solution.py:38
  20.8 0.3 fusion.234
  21.3 0.3 fusion.234
  21.8 0.3 fusion.234
  22.3 0.3 fusion.234
  23.1 1.6 while.58
  25.6 4.9 %while.56 = (s32[]{:T(128)}, bf16[4,8,8,64]{3,2,1,0:T(8,128)(2,1)S(1)}, bf16[4,8,8,64]{3,2,1,0:T(8,128)(2,1)S(1)}, bf16[4,8,8,64]{3,2,1,0:T(8,128)(2,1)S(1)}, bf...) while((s32[]{:T(128)}, ...), condition=%wide.region_5.6_spmd, body=%wide.region_1.5_spmd.sunk | while | flops 549215 | bytes 388997 | solution.py:38
  31.3 0.7 fusion.99
  32.0 6.0 %all-to-all-start.1 = ((bf16[8,8,256]{2,0,1:T(8,128)(2,1)}), bf16[8,8,256]{2,0,1:T(8,128)(2,1)S(1)}, u32[]{:S(2)}, u32[]{:S(2)}) async-start(bf16[8,8,256]{2,0,1:T(8,128)(2,1)} %fusion.99), calls=%async_computation.1 | async-start | bytes 65536 | tf_op jit(solution)/shard_map/all_to_all | solution.py:61
  38.9 0.4 copy.103
  39.3 5.4 %all-to-all-done.1 = bf16[8,8,256]{2,0,1:T(8,128)(2,1)S(1)} async-done(((bf16[8,8,256]{2,0,1:T(8,128)(2,1)}), bf16[8,8,256]{2,0,1:T(8,128)(2,1)S(1)}, u32[]{:S(2)}, u32[]{:S(2)}) %all-to-all-start.1) | async-done | bytes 32800 | tf_op jit(solution)/shard_map/all_to_all | solution.py:61
  45.0 4.7 %while.57 = (s32[]{:T(128)}, bf16[4,1,64,64]{2,3,0,1:T(8,128)(2,1)S(1)}, bf16[4,1,64,64]{2,3,0,1:T(8,128)(2,1)S(1)}, bf16[4,1,64,64]{2,3,1,0:T(8,128)(2,1)S(1)},...) while((s32[]{:T(128)}, ...), condition=%wide.region_12.13_spmd, body=%wide.region_8.12_spmd.sunk | while | flops 2727939 | bytes 431237 | solution.py:38
  49.8 0.4 convolution_convert_fusion.11
  50.7 0.4 copy.102
  51.1 1.7 pad_maximum_fusion
  52.9 0.6 copy-done.4
  53.6 0.6 dynamic-slice.2
  54.2 0.6 dynamic-slice
  54.8 0.4 fusion.97
  55.2 0.7 fusion.117
  55.9 72.8 %all-reduce.15.cloned.1.call-done = bf16[2,4,8,8192]{3,1,0,2:T(4,128)(2,1)} async-done(((bf16[2,4,8,8192]{3,1,0,2:T(4,128)(2,1)}), bf16[2,4,8,8192]{3,1,0,2:T(4,128)(2,1)}) %all-reduce.15.cloned.1.call-update) | async-done | bytes 1048592
  128.7 1.6 dynamic-slice_bitcast_fusion.8
  130.3 0.8 copy.104
  131.1 39.6 %psum.7 = f32[2,256]{1,0:T(2,128)} all-reduce(f32[2,256]{1,0:T(2,128)S(1)} %maximum_multiply_fusion), channel_id=1, replica_groups=mesh['dp'=4,'seq'=8] {'dp','seq'}, use_global_device_ids=true, to_apply=%region_26.27 | all-reduce | flops 512 | bytes 4096 | tf_op jit(solution)/shard_map/psum | solution.py:80
  170.7 2.0 %bitcast_convert_fusion = f32[2,8192]{1,0:T(2,128)} fusion(bf16[2,4,8192]{2,0,1:T(2,128)(2,1)} %all-reduce.17.cloned.1.call-done, u32[]{:T(128)} %bitcast.79), kind=kLoop, calls=%fused_computation.171 | loop fusion | flops 16384 | bytes 98308 | tf_op jit(solution)/shard_map/reshape | solution.py:78
  (174 shorter events, 16.1 us)
Async XLA Ops:
  9.7 7.4 %copy-start = (bf16[1,8,8,256]{3,2,1,0:T(8,128)(2,1)S(1)}, bf16[1,8,8,256]{3,2,1,0:T(8,128)(2,1)}, u32[]{:S(2)}) copy-start(bf16[1,8,8,256]{3,2,1,0:T(8,128)(2,1)} %param.14) | copy-start | bytes 98308
  9.7 15.4 %all-to-all-start = ((bf16[8,2,1024]{2,1,0:T(2,128)(2,1)}), bf16[8,2,1024]{2,1,0:T(2,128)(2,1)S(1)}, u32[]{:S(2)}, u32[]{:S(2)}) async-start(bf16[8,2,1024]{2,1,0:T(2,128)(2,1)} %reshape.395), calls=%async_computation | async-start | bytes 65536 | tf_op jit(solution)/shard_map/all_to_all | solution.py:52
  17.3 0.8 copy-start.1
  18.0 0.7 copy-start.2
  32.0 12.7 %all-to-all-start.1 = ((bf16[8,8,256]{2,0,1:T(8,128)(2,1)}), bf16[8,8,256]{2,0,1:T(8,128)(2,1)S(1)}, u32[]{:S(2)}, u32[]{:S(2)}) async-start(bf16[8,8,256]{2,0,1:T(8,128)(2,1)} %fusion.99), calls=%async_computation.1 | async-start | bytes 65536 | tf_op jit(solution)/shard_map/all_to_all | solution.py:61
  38.0 90.8 %all-reduce.15.cloned.1.call-start = ((), (), s32[]{:S(2)}) async-start(), calls=%async_computation.2 | async-start | bytes 2097152
  52.9 117.9 %all-reduce.17.cloned.1.call-start = ((), (), s32[]{:S(2)}) async-start(), calls=%async_computation.3 | async-start | bytes 262144
  52.9 0.7 copy-start.4
  53.6 0.7 copy-start.3
Sparse Core Ops, SparseCore 0:
  53.0 75.6 all-reduce.14
  131.2 31.3 all-reduce.16
where the time goes:
time: 180 us
  waiting for transfers between devices  78.2 us (43%)
  blocking collectives  39.6 us (22%)
  between operations  14.4 us (8%)
  matrix products  13.7 us (8%)
  starting transfers between devices  13.5 us (8%)
  local copies, waits for them, and re-layouts  12 us (7%)
  other arithmetic  7.74 us (4%)
    unnamed x4, waiting for transfers between devices  72.8 us
    psum x1, blocking collectives, per_device(): lax.psum(jnp.stack([grad_gs, grad_gt]) * grad_factor, ('dp', 'seq'))  39.6 us
    all_to_all x1, starting transfers between devices, per_device(): lax.all_to_all(patch_major, 'seq', split_axis=0, concat_axis=1, tiled=True)  7.44 us
    all_to_all x1, starting transfers between devices, per_device(): lax.all_to_all(mid_grad, 'seq', split_axis=1, concat_axis=0, tiled=True)  5.99 us
    all_to_all x1, waiting for transfers between devices, per_device(): lax.all_to_all(mid_grad, 'seq', split_axis=1, concat_axis=0, tiled=True)  5.36 us
    dot_general x24, matrix products, one_head(): jnp.einsum('gqk,gke->gqe', probs, value_rows, preferred_element_type=jnp....  5.11 us
    dot_general x24, matrix products, one_head(): jnp.einsum('gqe,gke->gqk', query_rows, key_rows, preferred_element_type=j...  4.94 us
    unnamed x15, local copies, waits for them, and re-layouts  3.85 us
  transfers between devices with their start and end apart: 4, of which 2 were waited for; matrix products, arithmetic and copies ran while one was open for 6% of the time, Pallas kernels for 0%

commit v1 on v0

--- a/solution.py
+++ b/solution.py
@@ -77,7 +77,9 @@
         .astype(jnp.float32)
         .reshape(2, -1)
     )
-    gain_grads = lax.psum(jnp.stack([grad_gs, grad_gt]) * grad_factor, ("dp", "seq"))
+    gain_grads = jnp.sum(
+        lax.all_gather(jnp.stack([grad_gs, grad_gt]) * grad_factor, ("dp", "seq")), axis=0
+    )
     return (input_grad, weight_grads, gain_grads)
 
 

time: 180 us -> 207 us (1.15)
  blocking collectives: 39.6 us -> 66.2 us
    all_gather x0 -> x1, blocking collectives: none -> 66.2 us  [per_device(): lax.all_gather(jnp.stack([grad_gs, grad_gt]) * grad_factor, ('dp', 'seq'))]
    psum x1 -> x0, blocking collectives: 39.6 us -> none  [per_device(): lax.psum(jnp.stack([grad_gs, grad_gt]) * grad_factor, ('dp', 'seq'))]
  transfers between devices with their start and end apart: 4 -> 4, of which waited for: 2 -> 2; matrix products, arithmetic and copies ran while one was open for 6% -> 5% of each run, Pallas kernels for 0% -> 0%
where the time goes in v1:
time: 207 us
  waiting for transfers between devices  78.2 us (38%)
  blocking collectives  66.2 us (32%)
  between operations  14.4 us (7%)
  matrix products  13.7 us (7%)
  starting transfers between devices  13.5 us (7%)
  local copies, waits for them, and re-layouts  12 us (6%)
  other arithmetic  8.36 us (4%)
    unnamed x4, waiting for transfers between devices  72.8 us
    all_gather x1, blocking collectives, per_device(): lax.all_gather(jnp.stack([grad_gs, grad_gt]) * grad_factor, ('dp', 'seq'))  66.2 us
    all_to_all x1, starting transfers between devices, per_device(): lax.all_to_all(patch_major, 'seq', split_axis=0, concat_axis=1, tiled=True)  7.44 us
    all_to_all x1, starting transfers between devices, per_device(): lax.all_to_all(mid_grad, 'seq', split_axis=1, concat_axis=0, tiled=True)  5.99 us
    all_to_all x1, waiting for transfers between devices, per_device(): lax.all_to_all(mid_grad, 'seq', split_axis=1, concat_axis=0, tiled=True)  5.36 us
    dot_general x24, matrix products, one_head(): jnp.einsum('gqk,gke->gqe', probs, value_rows, preferred_element_type=jnp....  5.11 us
    dot_general x24, matrix products, one_head(): jnp.einsum('gqe,gke->gqk', query_rows, key_rows, preferred_element_type=j...  4.94 us
  transfers between devices with their start and end apart: 4, of which 2 were waited for; matrix products, arithmetic and copies ran while one was open for 5% of the time, Pallas kernels for 0%

profile of v1, /device:TPU:0, one launch (start us, length us, event | category | flops | bytes accessed | tf_op | source)
XLA Modules:
  0.0 206.9 jit_solution(7113433050615724808)
XLA Ops:
  7.2 0.5 broadcast.295
  7.7 1.4 reduce.34
  9.1 0.6 reshape.426
  9.7 7.4 %all-to-all-start = ((bf16[8,2,1024]{2,1,0:T(2,128)(2,1)}), bf16[8,2,1024]{2,1,0:T(2,128)(2,1)S(1)}, u32[]{:S(2)}, u32[]{:S(2)}) async-start(bf16[8,2,1024]{2,1,0:T(2,128)(2,1)} %reshape.426), calls=%async_computation | async-start | bytes 65536 | tf_op jit(solution)/shard_map/all_to_all | solution.py:52
  17.3 0.7 copy-done.1
  18.1 0.6 copy-done.2
  18.9 1.3 slice_bitcast_fusion.1
  20.6 2.0 while.59
  20.8 0.3 fusion.234
  21.8 0.3 fusion.234
  22.3 0.3 fusion.234
  23.1 1.6 while.58
  25.6 4.9 %while.56 = (s32[]{:T(128)}, bf16[4,8,8,64]{3,2,1,0:T(8,128)(2,1)S(1)}, bf16[4,8,8,64]{3,2,1,0:T(8,128)(2,1)S(1)}, bf16[4,8,8,64]{3,2,1,0:T(8,128)(2,1)S(1)}, bf...) while((s32[]{:T(128)}, ...), condition=%wide.region_5.6_spmd, body=%wide.region_1.5_spmd.sunk | while | flops 549215 | bytes 388997 | solution.py:38
  31.3 0.7 fusion.99
  32.0 6.0 %all-to-all-start.1 = ((bf16[8,8,256]{2,0,1:T(8,128)(2,1)}), bf16[8,8,256]{2,0,1:T(8,128)(2,1)S(1)}, u32[]{:S(2)}, u32[]{:S(2)}) async-start(bf16[8,8,256]{2,0,1:T(8,128)(2,1)} %fusion.99), calls=%async_computation.1 | async-start | bytes 65536 | tf_op jit(solution)/shard_map/all_to_all | solution.py:61
  38.9 0.4 copy.103
  39.3 5.4 %all-to-all-done.1 = bf16[8,8,256]{2,0,1:T(8,128)(2,1)S(1)} async-done(((bf16[8,8,256]{2,0,1:T(8,128)(2,1)}), bf16[8,8,256]{2,0,1:T(8,128)(2,1)S(1)}, u32[]{:S(2)}, u32[]{:S(2)}) %all-to-all-start.1) | async-done | bytes 32800 | tf_op jit(solution)/shard_map/all_to_all | solution.py:61
  45.0 4.7 %while.57 = (s32[]{:T(128)}, bf16[4,1,64,64]{2,3,0,1:T(8,128)(2,1)S(1)}, bf16[4,1,64,64]{2,3,0,1:T(8,128)(2,1)S(1)}, bf16[4,1,64,64]{2,3,1,0:T(8,128)(2,1)S(1)},...) while((s32[]{:T(128)}, ...), condition=%wide.region_12.13_spmd, body=%wide.region_8.12_spmd.sunk | while | flops 2727939 | bytes 431237 | solution.py:38
  49.8 0.4 convolution_convert_fusion.11
  50.7 0.4 copy.102
  51.1 1.7 pad_maximum_fusion
  52.9 0.6 copy-done.4
  53.6 0.6 dynamic-slice.2
  54.2 0.6 dynamic-slice
  54.8 0.4 fusion.97
  55.2 0.7 fusion.117
  55.9 72.8 %all-reduce.15.cloned.1.call-done = bf16[2,4,8,8192]{3,1,0,2:T(4,128)(2,1)} async-done(((bf16[2,4,8,8192]{3,1,0,2:T(4,128)(2,1)}), bf16[2,4,8,8192]{3,1,0,2:T(4,128)(2,1)}) %all-reduce.15.cloned.1.call-update) | async-done | bytes 1048592
  128.7 1.6 dynamic-slice_bitcast_fusion.8
  130.3 0.8 copy.104
  131.1 66.2 %all_gather.4 = f32[32,2,256]{2,1,0:T(2,128)S(1)} all-gather(f32[1,2,256]{2,1,0:T(2,128)S(1)} %maximum_multiply_fusion), channel_id=1, replica_groups=mesh['dp'=4,'seq'=8] {'dp','seq'}, dimensions={0}, use_global_device_ids=true | all-gather | bytes 67584 | tf_op jit(solution)/shard_map/all_gather | solution.py:81
  197.4 0.6 reduce_sum.159
  198.0 2.0 bitcast_convert_fusion
  (175 shorter events, 16.5 us)
Async XLA Ops:
  9.7 7.4 %copy-start = (bf16[1,8,8,256]{3,2,1,0:T(8,128)(2,1)S(1)}, bf16[1,8,8,256]{3,2,1,0:T(8,128)(2,1)}, u32[]{:S(2)}) copy-start(bf16[1,8,8,256]{3,2,1,0:T(8,128)(2,1)} %param.14) | copy-start | bytes 98308
  9.7 15.4 %all-to-all-start = ((bf16[8,2,1024]{2,1,0:T(2,128)(2,1)}), bf16[8,2,1024]{2,1,0:T(2,128)(2,1)S(1)}, u32[]{:S(2)}, u32[]{:S(2)}) async-start(bf16[8,2,1024]{2,1,0:T(2,128)(2,1)} %reshape.426), calls=%async_computation | async-start | bytes 65536 | tf_op jit(solution)/shard_map/all_to_all | solution.py:52
  17.3 0.8 copy-start.1
  18.0 0.7 copy-start.2
  32.0 12.7 %all-to-all-start.1 = ((bf16[8,8,256]{2,0,1:T(8,128)(2,1)}), bf16[8,8,256]{2,0,1:T(8,128)(2,1)S(1)}, u32[]{:S(2)}, u32[]{:S(2)}) async-start(bf16[8,8,256]{2,0,1:T(8,128)(2,1)} %fusion.99), calls=%async_computation.1 | async-start | bytes 65536 | tf_op jit(solution)/shard_map/all_to_all | solution.py:61
  38.0 90.8 %all-reduce.15.cloned.1.call-start = ((), (), s32[]{:S(2)}) async-start(), calls=%async_computation.2 | async-start | bytes 2097152
  52.9 145.1 %all-reduce.17.cloned.1.call-start = ((), (), s32[]{:S(2)}) async-start(), calls=%async_computation.3 | async-start | bytes 262144
  52.9 0.7 copy-start.4
  53.6 0.7 copy-start.3
Sparse Core Ops, SparseCore 0:
  53.0 75.6 all-reduce.14
  131.2 31.3 all-reduce.16
